TPU v7x, 128 devices: a whole 4x4x4 slice. The times are simulated.
128 devices in a mesh: expert: 8 (over x, core), fsdp: 16 (over z, y).
Axes of the slice: x: 4, y: 4, z: 4, core: 2. Of those that a mesh axis runs over, the one named last changes fastest.
Arguments:
- tokens: bfloat16 [16384, 1536], P(('expert', 'fsdp')), may hold values from -6 to 6
- gate_probs: float32 [16384, 2], P(('expert', 'fsdp')), may hold values from 0.1 to 1
- expert_ids: int32 [16384, 2], P(('expert', 'fsdp')), may hold values from 0 to 7, all different within a row; in each aligned block of 128 rows (0 to 127, 128 to 255, ...) at most 32 rows name the same one
- cotangent: bfloat16 [16384, 1536], P(('expert', 'fsdp')), may hold values from -0.59765625 to 0.59765625
- gate_weight: bfloat16 [8, 1536, 2048], P('expert', None, 'fsdp'), may hold values from -0.15625 to 0.15625
- up_weight: bfloat16 [8, 1536, 2048], P('expert', None, 'fsdp'), may hold values from -0.15625 to 0.15625
- down_weight: bfloat16 [8, 2048, 1536], P('expert', 'fsdp'), may hold values from -0.125 to 0.125
Outputs:
- mixed: bfloat16 [16384, 1536], P(('expert', 'fsdp'))
- d_tokens: bfloat16 [16384, 1536], P(('expert', 'fsdp'))
- d_gates: float32 [16384, 2], P(('expert', 'fsdp'))
- d_gate_weight: float32 [8, 1536, 2048], P('expert', None, 'fsdp')
- d_up_weight: float32 [8, 1536, 2048], P('expert', None, 'fsdp')
- d_down_weight: float32 [8, 2048, 1536], P('expert', 'fsdp')
Inputs may be any that keep to these rules, and one draw needn't show every extreme that they name: `expert_ids`: the two experts of a token differ. In the 128 rows of one device every expert is named exactly 32 times.
All inputs are finite; a program needn't handle non-finite values.
Results may differ from a plain program's by a relative error of at most 0.015.
Values may be sent and summed in bfloat16 or wider, within the bound.
A program may use at most 192 MiB of HBM per device.

v0:
```python
import jax
import jax.numpy as jnp
from jax import lax
from jax.sharding import PartitionSpec as P


def build_dispatch(expert_ids, capacity, num_experts):
    flat_ids = expert_ids.reshape(-1)
    onehot = (flat_ids[:, None] == jnp.arange(num_experts, dtype=jnp.int32)[None, :]).astype(
        jnp.int32
    )
    before = jnp.cumsum(onehot, axis=0) - onehot
    slot_pos = jnp.sum(before * onehot, axis=1)
    target = flat_ids * capacity + slot_pos
    return (jnp.arange(num_experts * capacity, dtype=jnp.int32)[:, None] == target[None, :]).astype(
        jnp.bfloat16
    )


def deliver(buffer):
    arrived = lax.all_to_all(buffer, "expert", split_axis=0, concat_axis=0, tiled=True)
    arrived = lax.all_gather(arrived[None], "fsdp", axis=0, tiled=True)
    return arrived.reshape(-1, buffer.shape[-1])


def bring_back(partial_value, num_experts, capacity):
    columns = partial_value.shape[-1]
    blocks = partial_value.astype(jnp.bfloat16).reshape(-1, num_experts, capacity, columns)
    summed = lax.psum_scatter(blocks, "fsdp", scatter_dimension=0, tiled=True).astype(jnp.float32)
    result = lax.all_to_all(
        summed[0].astype(jnp.bfloat16), "expert", split_axis=0, concat_axis=0, tiled=True
    )
    return result.reshape(num_experts * capacity, columns)


def per_device(tokens, gate_probs, expert_ids, cotangent, gate_weight, up_weight, down_weight):
    tok_rows, columns = tokens.shape
    num_experts = lax.axis_size("expert")
    capacity = 2 * tok_rows // num_experts
    dispatch = build_dispatch(expert_ids, capacity, num_experts)
    token_map = jnp.sum(dispatch.reshape(num_experts * capacity, tok_rows, 2), axis=2)
    contract_rows = (((0,), (0,)), ((), ()))
    contract_cols = (((1,), (1,)), ((), ()))
    outgoing = jnp.dot(token_map, tokens, preferred_element_type=jnp.float32).astype(jnp.bfloat16)
    cot_wide = cotangent.astype(jnp.float32)
    scaled = (
        (gate_probs[:, :, None] * cot_wide[:, None, :])
        .astype(jnp.bfloat16)
        .reshape(2 * tok_rows, columns)
    )
    grad_out = jnp.dot(dispatch, scaled, preferred_element_type=jnp.float32).astype(jnp.bfloat16)
    token_slots = outgoing.reshape(num_experts, capacity, columns)
    grad_slots = grad_out.reshape(num_experts, capacity, columns)
    rows_in = deliver(token_slots)
    w_gate = gate_weight[0]
    w_up = up_weight[0]
    w_down = down_weight[0]
    pre_gate = jnp.dot(rows_in, w_gate, preferred_element_type=jnp.float32)
    pre_up = jnp.dot(rows_in, w_up, preferred_element_type=jnp.float32)
    sigmoid_gate = jax.nn.sigmoid(pre_gate)
    hidden = (pre_gate * sigmoid_gate * pre_up).astype(jnp.bfloat16)
    partial_value = jnp.dot(hidden, w_down, preferred_element_type=jnp.float32)
    expert_out = bring_back(partial_value, num_experts, capacity)
    per_pair = lax.dot_general(
        dispatch, expert_out, contract_rows, preferred_element_type=jnp.float32
    ).reshape(tok_rows, 2, columns)
    mixed = jnp.sum(gate_probs[:, :, None] * per_pair, axis=1).astype(jnp.bfloat16)
    d_gates = jnp.sum(cot_wide[:, None, :] * per_pair, axis=2)
    grad_rows = deliver(grad_slots)
    d_hidden = lax.dot_general(grad_rows, w_down, contract_cols, preferred_element_type=jnp.float32)
    d_pre_gate = (
        d_hidden * pre_up * sigmoid_gate * (1.0 + pre_gate * (1.0 - sigmoid_gate))
    ).astype(jnp.bfloat16)
    d_pre_up = (d_hidden * pre_gate * sigmoid_gate).astype(jnp.bfloat16)
    d_down = lax.dot_general(hidden, grad_rows, contract_rows, preferred_element_type=jnp.float32)
    d_gate_w = lax.dot_general(
        rows_in, d_pre_gate, contract_rows, preferred_element_type=jnp.float32
    )
    d_up_w = lax.dot_general(rows_in, d_pre_up, contract_rows, preferred_element_type=jnp.float32)
    back_partial = lax.dot_general(
        d_pre_gate, w_gate, contract_cols, preferred_element_type=jnp.float32
    )
    back_partial = back_partial + lax.dot_general(
        d_pre_up, w_up, contract_cols, preferred_element_type=jnp.float32
    )
    d_rows = bring_back(back_partial, num_experts, capacity)
    d_tokens = lax.dot_general(
        token_map, d_rows, contract_rows, preferred_element_type=jnp.float32
    ).astype(jnp.bfloat16)
    return (mixed, d_tokens, d_gates, d_gate_w[None], d_up_w[None], d_down[None])


def solution(mesh):
    placed = (
        P(("expert", "fsdp"), None),
        P(("expert", "fsdp"), None),
        P(("expert", "fsdp"), None),
        P(("expert", "fsdp"), None),
        P("expert", None, "fsdp"),
        P("expert", None, "fsdp"),
        P("expert", "fsdp", None),
    )
    return jax.shard_map(
        per_device,
        mesh=mesh,
        in_specs=placed,
        out_specs=(
            P(("expert", "fsdp"), None),
            P(("expert", "fsdp"), None),
            P(("expert", "fsdp"), None),
            P("expert", None, "fsdp"),
            P("expert", None, "fsdp"),
            P("expert", "fsdp", None),
        ),
        check_vma=False,
    )
```

profile of v0, /device:TPU:1, one launch (start us, length us, event | category | flops | bytes accessed | tf_op | source)
XLA Modules:
  0.0 466.0 jit_solution(14920518914551212987)
XLA Ops:
  7.2 0.0 copy-start
  7.2 0.0 copy-start.12
  7.2 0.0 copy-start.3
  7.2 0.0 all-gather.5.cloned.1.call-start
  7.2 0.9 copy.36
  8.1 0.1 reshape.107
  8.3 0.1 eq.62
  8.4 0.6 reduce-window.6
  9.0 0.2 slice_reduce_fusion
  9.3 0.1 fusion.17
  9.4 0.1 reduce_sum.42
  9.5 0.1 copy.38
  9.6 0.7 multiply_add_fusion
  10.3 0.0 copy-start.9
  10.3 0.6 copy-done.9
  10.9 1.3 convolution_convert_fusion.1
  12.3 17.8 %all_to_all.20 = bf16[8,32,1536]{2,1,0:T(8,128)(2,1)} all-to-all(bf16[8,32,1536]{2,1,0:T(8,128)(2,1)S(1)} %bitcast.70), channel_id=1, replica_groups=mesh['expert'=8,'fsdp'=16] {'expert'}, dimensions={0} | all-to-all | bytes 1572864 | tf_op jit(solution)/shard_map/all_to_all | solution.py:21
  30.1 0.0 all-gather.5.cloned.1.call-update
  30.1 0.0 all-gather.7.cloned.1.call-start
  30.2 0.0 copy-done.12
  30.2 0.1 copy.40
  30.3 0.1 mul.83
  30.5 0.0 copy-done.3
  30.5 0.4 mul.85.clone
  30.9 1.1 mul.86
  32.0 0.0 copy-start.2
  32.0 0.5 convolution_convert_fusion.2
  32.5 16.3 %all_to_all.21 = bf16[8,32,1536]{2,1,0:T(8,128)(2,1)} all-to-all(bf16[8,32,1536]{2,1,0:T(8,128)(2,1)S(1)} %bitcast.71), channel_id=1, replica_groups=mesh['expert'=8,'fsdp'=16] {'expert'}, dimensions={0} | all-to-all | bytes 1572864 | tf_op jit(solution)/shard_map/all_to_all | solution.py:21
  48.7 0.0 all-gather.7.cloned.1.call-update
  48.7 0.2 reduce-scatter.9.cloned.1.call-start
  49.0 72.0 %all-gather.5.cloned.1.call-done = bf16[128,32,1536]{2,1,0:T(8,128)(2,1)} async-done(((bf16[8,32,1536]{2,1,0:T(8,128)(2,1)}), bf16[128,32,1536]{2,1,0:T(8,128)(2,1)}) %all-gather.5.cloned.1.call-update) | async-done | bytes 12582928 | tf_op jit(solution)/shard_map/all_gather | solution.py:22
  120.9 0.0 copy-done.2
  120.9 7.9 %fusion.5 = f32[4096,128]{1,0:T(8,128)} fusion(bf16[4096,1536]{1,0:T(8,128)(2,1)} %bitcast.63, bf16[1,1536,128]{2,1,0:T(8,128)(2,1)S(1)} %copy-done.2), kind=kOutput, calls=%fused_computation.20 | convolution fusion | flops 1610612736 | bytes 15073280 | tf_op jit(solution)/shard_map/dot_general | solution.py:59
  128.8 1.1 copy-done.1
  129.9 0.0 copy-done.5
  129.9 4.8 %fusion.9 = f32[4096,128]{1,0:T(8,128)} fusion(bf16[4096,1536]{1,0:T(8,128)(2,1)S(1)} %bitcast.66, bf16[1,1536,128]{2,1,0:T(8,128)(2,1)S(1)} %copy-done.5), kind=kOutput, calls=%fused_computation.24 | convolution fusion | flops 1610612736 | bytes 15073280 | tf_op jit(solution)/shard_map/dot_general | solution.py:58
  134.6 78.0 %all-gather.7.cloned.1.call-done = bf16[128,32,1536]{2,1,0:T(8,128)(2,1)} async-done(((bf16[8,32,1536]{2,1,0:T(8,128)(2,1)}), bf16[128,32,1536]{2,1,0:T(8,128)(2,1)}) %all-gather.7.cloned.1.call-update) | async-done | bytes 12582928 | tf_op jit(solution)/shard_map/all_gather | solution.py:22
  212.6 0.0 copy-done
  212.6 9.6 %multiply_convert_fusion = (bf16[4096,128]{1,0:T(8,128)(2,1)S(1)}, bf16[4096,128]{1,0:T(8,128)(2,1)S(1)}, bf16[4096,128]{1,0:T(8,128)(2,1)S(1)}) fusion(f32[4096,128]{1,0:T(8,128)} %fusion.9, f32[4096,128]{1,0:T(8,128)} %fusion.5, bf16[4096,1536]{1,0:T(8,128)(2,1)} %bitcast.67, bf16[1,128,1536]{2,1,0:T(8,128)(2,1)S(1)} %copy-done), kind=kOutput, calls=%fused_computation.8 | convolution fusion | flops 1619001344 | bytes 20316160 | tf_op jit(solution)/shard_map/dot_general | solution.py:70
  222.2 0.0 copy-start.6
  222.2 10.1 %fusion.7 = f32[4096,1536]{1,0:T(8,128)} fusion(bf16[4096,128]{1,0:T(8,128)(2,1)S(1)} %get-tuple-element.9, bf16[1,1536,128]{2,1,0:T(8,128)(2,1)S(1)} %copy-done.5), kind=kOutput, calls=%fused_computation.22 | convolution fusion | flops 1610612736 | bytes 26607616 | tf_op jit(solution)/shard_map/dot_general | solution.py:80
  232.3 0.0 copy-done.6
  232.4 14.7 %add_convert_fusion = bf16[4096,1536]{1,0:T(8,128)(2,1)} fusion(f32[4096,1536]{1,0:T(8,128)} %fusion.7, bf16[4096,128]{1,0:T(8,128)(2,1)S(1)} %get-tuple-element.8, bf16[1,1536,128]{2,1,0:T(8,128)(2,1)S(1)} %copy-done.2), kind=kOutput, calls=%fused_computation | convolution fusion | flops 1623195648 | bytes 39190528 | tf_op jit(solution)/shard_map/dot_general | solution.py:83
  247.1 0.0 reduce-scatter.9.cloned.1.call-update
  247.1 0.3 reduce-scatter.7.cloned.1.call-start
  247.4 6.4 %convolution_convert_fusion = bf16[4096,1536]{1,0:T(8,128)(2,1)} fusion(bf16[4096,128]{1,0:T(8,128)(2,1)S(1)} %get-tuple-element.10, bf16[1,128,1536]{2,1,0:T(8,128)(2,1)S(1)} %copy-done), kind=kOutput, calls=%fused_computation.1 | convolution fusion | flops 1616904192 | bytes 14024704 | tf_op jit(solution)/shard_map/dot_general | solution.py:62
  253.7 0.0 reduce-scatter.7.cloned.1.call-update
  253.7 1.0 copy-done.4
  254.7 1.0 convert_element_type.65
  255.7 0.1 iota_compare_fusion.2
  255.8 0.7 eq.68
  256.5 7.5 %convolution_bitcast_fusion.1 = f32[1,1536,128]{2,1,0:T(8,128)} fusion(bf16[4096,1536]{1,0:T(8,128)(2,1)} %bitcast.64, bf16[4096,128]{1,0:T(8,128)(2,1)S(1)} %get-tuple-element.8), kind=kOutput, calls=%fused_computation.5 | convolution fusion | flops 1610612736 | bytes 14417920 | tf_op jit(solution)/shard_map/dot_general | solution.py:79
  264.0 77.9 %reduce-scatter.9.cloned.1.call-done = bf16[1,8,32,1536]{3,2,1,0:T(8,128)(2,1)} async-done(((bf16[16,8,32,1536]{3,2,1,0:T(8,128)(2,1)}), bf16[1,8,32,1536]{3,2,1,0:T(8,128)(2,1)}) %reduce-scatter.9.cloned.1.call-update) | async-done | bytes 786448
  341.9 5.4 %all-to-all-start.3 = ((bf16[8,32,1536]{2,1,0:T(8,128)(2,1)}), bf16[8,32,1536]{2,1,0:T(8,128)(2,1)S(1)}, u32[]{:S(2)}, u32[]{:S(2)}) async-start(bf16[8,32,1536]{2,1,0:T(8,128)(2,1)} %bitcast.73), calls=%async_computation.3 | async-start | bytes 1572864 | tf_op jit(solution)/shard_map/all_to_all | solution.py:30
  347.3 0.0 copy-done.7
  347.3 7.3 %convolution_bitcast_fusion.2 = f32[1,1536,128]{2,1,0:T(8,128)} fusion(bf16[4096,1536]{1,0:T(8,128)(2,1)} %bitcast.65, bf16[4096,128]{1,0:T(8,128)(2,1)S(1)} %copy-done.7), kind=kOutput, calls=%fused_computation.6 | convolution fusion | flops 1610612736 | bytes 14417920 | tf_op jit(solution)/shard_map/dot_general | solution.py:76
  354.6 84.7 %reduce-scatter.7.cloned.1.call-done = bf16[1,8,32,1536]{3,2,1,0:T(8,128)(2,1)} async-done(((bf16[16,8,32,1536]{3,2,1,0:T(8,128)(2,1)}), bf16[1,8,32,1536]{3,2,1,0:T(8,128)(2,1)}) %reduce-scatter.7.cloned.1.call-update) | async-done | bytes 786448
  439.3 0.0 all-to-all-done.3
  439.4 5.4 %all-to-all-start.1 = ((bf16[8,32,1536]{2,1,0:T(8,128)(2,1)}), bf16[8,32,1536]{2,1,0:T(8,128)(2,1)}, u32[]{:S(2)}, u32[]{:S(2)}) async-start(bf16[8,32,1536]{2,1,0:T(8,128)(2,1)} %bitcast.72), calls=%async_computation.1 | async-start | bytes 1572864 | tf_op jit(solution)/shard_map/all_to_all | solution.py:30
  444.8 7.4 %convolution_bitcast_fusion = f32[1,128,1536]{2,1,0:T(8,128)} fusion(bf16[4096,128]{1,0:T(8,128)(2,1)S(1)} %get-tuple-element.10, bf16[4096,1536]{1,0:T(8,128)(2,1)} %bitcast.68), kind=kOutput, calls=%fused_computation.4 | convolution fusion | flops 1610612736 | bytes 14417920 | tf_op jit(solution)/shard_map/dot_general | solution.py:75
  452.2 0.0 copy-done.10
  452.2 1.0 convolution_convert_fusion.3
  453.2 3.8 all-to-all-done.1
  457.0 2.5 multiply_reduce_fusion
  (14 shorter events, 0.1 us)
Async XLA Ops:
  7.2 205.4 %copy-start = (bf16[1,128,1536]{2,1,0:T(8,128)(2,1)S(1)}, bf16[1,128,1536]{2,1,0:T(8,128)(2,1)}, u32[]{:S(2)}) copy-start(bf16[1,128,1536]{2,1,0:T(8,128)(2,1)} %param.13) | copy-start | bytes 1179652
  7.2 23.0 %copy-start.12 = (f32[128,2]{0,1:T(2,128)S(1)}, f32[128,2]{0,1:T(2,128)}, u32[]{:S(2)}) copy-start(f32[128,2]{0,1:T(2,128)} %param.8) | copy-start | bytes 3076
  7.2 23.3 %copy-start.3 = (bf16[128,1536]{1,0:T(8,128)(2,1)S(1)}, bf16[128,1536]{1,0:T(8,128)(2,1)}, u32[]{:S(2)}) copy-start(bf16[128,1536]{1,0:T(8,128)(2,1)} %param.10) | copy-start | bytes 1179652
  7.2 113.7 %all-gather.5.cloned.1.call-start = ((), (), s32[]{:S(2)}) async-start(), calls=%async_computation.6 | async-start | bytes 13369344 | tf_op jit(solution)/shard_map/all_gather | solution.py:22
  10.3 0.6 copy-start.9
  30.1 182.5 %all-gather.7.cloned.1.call-start = ((), (), s32[]{:S(2)}) async-start(), calls=%async_computation.7 | async-start | bytes 13369344 | tf_op jit(solution)/shard_map/all_gather | solution.py:22
  32.0 89.0 %copy-start.2 = (bf16[1,1536,128]{2,1,0:T(8,128)(2,1)S(1)}, bf16[1,1536,128]{2,1,0:T(8,128)(2,1)}, u32[]{:S(2)}) copy-start(bf16[1,1536,128]{2,1,0:T(8,128)(2,1)} %param.12) | copy-start | bytes 1179652
  48.7 293.1 %reduce-scatter.9.cloned.1.call-start = ((), (), s32[]{:S(2)}) async-start(), calls=%async_computation.9 | async-start | bytes 13369344
  120.9 8.9 %copy-start.1 = (bf16[128,32,1536]{2,1,0:T(8,128)(2,1)S(1)}, bf16[128,32,1536]{2,1,0:T(8,128)(2,1)}, u32[]{:S(2)}) copy-start(bf16[128,32,1536]{2,1,0:T(8,128)(2,1)} %all-gather.5.cloned.1.call-done) | copy-start | bytes 37748740
  120.9 8.9 %copy-start.5 = (bf16[1,1536,128]{2,1,0:T(8,128)(2,1)S(1)}, bf16[1,1536,128]{2,1,0:T(8,128)(2,1)}, u32[]{:S(2)}) copy-start(bf16[1,1536,128]{2,1,0:T(8,128)(2,1)} %param.11) | copy-start | bytes 1179652
  222.2 10.1 %copy-start.6 = (bf16[4096,128]{1,0:T(8,128)(2,1)}, bf16[4096,128]{1,0:T(8,128)(2,1)S(1)}, u32[]{:S(2)}) copy-start(bf16[4096,128]{1,0:T(8,128)(2,1)S(1)} %get-tuple-element.9) | copy-start | bytes 3145732
  247.1 192.3 %reduce-scatter.7.cloned.1.call-start = ((), (), s32[]{:S(2)}) async-start(), calls=%async_computation.8 | async-start | bytes 13369344
  253.7 1.0 copy-start.4
  256.5 90.8 %copy-start.7 = (bf16[4096,128]{1,0:T(8,128)(2,1)S(1)}, bf16[4096,128]{1,0:T(8,128)(2,1)}, u32[]{:S(2)}) copy-start(bf16[4096,128]{1,0:T(8,128)(2,1)} %copy-done.6) | copy-start | bytes 3145732
  341.9 97.5 %all-to-all-start.3 = ((bf16[8,32,1536]{2,1,0:T(8,128)(2,1)}), bf16[8,32,1536]{2,1,0:T(8,128)(2,1)S(1)}, u32[]{:S(2)}, u32[]{:S(2)}) async-start(bf16[8,32,1536]{2,1,0:T(8,128)(2,1)} %bitcast.73), calls=%async_computation.3 | async-start | bytes 1572864 | tf_op jit(solution)/shard_map/all_to_all | solution.py:30
  439.4 17.7 %all-to-all-start.1 = ((bf16[8,32,1536]{2,1,0:T(8,128)(2,1)}), bf16[8,32,1536]{2,1,0:T(8,128)(2,1)}, u32[]{:S(2)}, u32[]{:S(2)}) async-start(bf16[8,32,1536]{2,1,0:T(8,128)(2,1)} %bitcast.72), calls=%async_computation.1 | async-start | bytes 1572864 | tf_op jit(solution)/shard_map/all_to_all | solution.py:30
  444.8 7.4 %copy-start.10 = (bf16[256,128]{1,0:T(8,128)(2,1)S(1)}, bf16[256,128]{1,0:T(8,128)(2,1)}, u32[]{:S(2)}) copy-start(bf16[256,128]{1,0:T(8,128)(2,1)} %copy-done.9) | copy-start | bytes 196612
  444.8 12.3 %copy-start.8 = (f32[128,1536]{1,0:T(8,128)S(1)}, f32[128,1536]{1,0:T(8,128)}, u32[]{:S(2)}) copy-start(f32[128,1536]{1,0:T(8,128)} %convert_element_type.65) | copy-start | bytes 2359300
  444.8 12.3 %copy-start.11 = (pred[128,2,256]{2,1,0:T(4,128)(4,1)S(1)}, pred[128,2,256]{2,1,0:T(4,128)(4,1)}, u32[]{:S(2)}) copy-start(pred[128,2,256]{2,1,0:T(4,128)(4,1)} %eq.68) | copy-start | bytes 196612
Sparse Core Ops, SparseCore 0:
  30.3 90.6 all-gather.4
  123.1 89.4 all-gather.6
  247.2 94.6 reduce-scatter.8
  345.2 94.1 reduce-scatter.6
where the time goes:
time: 467 us; the launch traced here: 466 us
  waiting for transfers between devices  316 us (68%)
  matrix products  81 us (17%)
  blocking collectives  34.1 us (7%)
  between operations  13.9 us (3%)
  starting transfers between devices  11.4 us (2%)
  local copies, waits for them, and re-layouts  6.75 us (1%)
    unnamed x6, waiting for transfers between devices  163 us
    all_gather x2, waiting for transfers between devices, deliver(): arrived = lax.all_gather(arrived[None], 'fsdp', axis=0, tiled=True)  150 us
    all_to_all x2, blocking collectives, deliver(): lax.all_to_all(buffer, 'expert', split_axis=0, concat_axis=0, tiled=True)  34.1 us
    dot_general x1, matrix products, per_device(): lax.dot_general(d_pre_up, w_up, contract_cols, preferred_element_type=jnp...  14.7 us
    all_to_all x2, starting transfers between devices, bring_back(): lax.all_to_all(summed[0].astype(jnp.bfloat16), 'expert', split_axis=0, co...  10.8 us
    dot_general x1, matrix products, per_device(): lax.dot_general(d_pre_gate, w_gate, contract_cols, preferred_element_type...  10.1 us
    dot_general x1, matrix products, per_device(): lax.dot_general(grad_rows, w_down, contract_cols, preferred_element_type=...  9.6 us
  transfers between devices with their start and end apart: 6, of which 5 were waited for; matrix products, arithmetic and copies ran while one was open for 10% of the time, Pallas kernels for 0%

commit v1 on v0

--- a/solution.py
+++ b/solution.py
@@ -19,7 +19,16 @@
 
 def deliver(buffer):
     arrived = lax.all_to_all(buffer, "expert", split_axis=0, concat_axis=0, tiled=True)
-    arrived = lax.all_gather(arrived[None], "fsdp", axis=0, tiled=True)
+    payload = arrived[None]
+    arrived = jnp.concatenate(
+        lax.all_to_all(
+            jnp.stack(lax.axis_size("fsdp") * [payload]),
+            split_axis=0,
+            axis_name="fsdp",
+            concat_axis=0,
+        ),
+        axis=0,
+    )
     return arrived.reshape(-1, buffer.shape[-1])
 
 

time: 467 us -> 650 us (1.39)
  blocking collectives: 34.1 us -> 163 us
  waiting for transfers between devices: 316 us -> 343 us
  local copies, waits for them, and re-layouts: 6.75 us -> 19.1 us
  starting transfers between devices: 11.4 us -> 22.2 us
    all_to_all x0 -> x2, waiting for transfers between devices: none -> 176 us  [the longest x1 166 us: deliver(): lax.all_to_all(jnp.stack(lax.axis_size('fsdp') * [payload]), split_axis=0...]
    all_gather x2 -> x0, waiting for transfers between devices: 150 us -> none  [deliver(): arrived = lax.all_gather(arrived[None], 'fsdp', axis=0, tiled=True)]
    all_to_all x0 -> x1, blocking collectives: none -> 147 us  [deliver(): lax.all_to_all(jnp.stack(lax.axis_size('fsdp') * [payload]), split_axis=0...]
    all_to_all x2 -> x1, blocking collectives: 34.1 us -> 15.5 us  [deliver(): lax.all_to_all(buffer, 'expert', split_axis=0, concat_axis=0, tiled=True)]
    another operation x1 -> x3, local copies, waits for them, and re-layouts: 0.01 us -> 13.4 us  [the longest x2 13.4 us: deliver(): jnp.stack(lax.axis_size('fsdp') * [payload])]
    all_to_all x0 -> x2, starting transfers between devices: none -> 10.9 us  [the longest x1 5.79 us: deliver(): lax.all_to_all(buffer, 'expert', split_axis=0, concat_axis=0, tiled=True)]
    unnamed x6 -> x4, waiting for transfers between devices: 163 us -> 163 us
  transfers between devices with their start and end apart: 6 -> 6, of which waited for: 5 -> 5; matrix products, arithmetic and copies ran while one was open for 10% -> 8% of each run, Pallas kernels for 0% -> 0%
where the time goes in v1:
time: 650 us; the launch traced here: 649 us
  waiting for transfers between devices  343 us (53%)
  blocking collectives  163 us (25%)
  matrix products  85.3 us (13%)
  starting transfers between devices  22.2 us (3%)
  local copies, waits for them, and re-layouts  19.1 us (3%)
  between operations  14.2 us (2%)
    all_to_all x1, waiting for transfers between devices, deliver(): lax.all_to_all(jnp.stack(lax.axis_size('fsdp') * [payload]), split_axis=0...  166 us
    unnamed x4, waiting for transfers between devices  163 us
    all_to_all x1, blocking collectives, deliver(): lax.all_to_all(jnp.stack(lax.axis_size('fsdp') * [payload]), split_axis=0...  147 us
    all_to_all x1, blocking collectives, deliver(): lax.all_to_all(buffer, 'expert', split_axis=0, concat_axis=0, tiled=True)  15.5 us
    dot_general x1, matrix products, per_device(): lax.dot_general(d_pre_up, w_up, contract_cols, preferred_element_type=jnp...  14.7 us
    another operation x2, local copies, waits for them, and re-layouts, deliver(): jnp.stack(lax.axis_size('fsdp') * [payload])  13.4 us
  transfers between devices with their start and end apart: 6, of which 5 were waited for; matrix products, arithmetic and copies ran while one was open for 8% of the time, Pallas kernels for 0%

profile of v1, /device:TPU:1, one launch (start us, length us, event | category | flops | bytes accessed | tf_op | source)
XLA Modules:
  0.0 649.2 jit_solution(12513221986421282020)
XLA Ops:
  7.2 0.0 copy-start
  7.2 0.0 copy-start.11
  7.2 0.0 copy-start.2
  7.2 0.9 copy.36
  8.1 0.1 reshape.105
  8.2 0.1 eq.62
  8.4 0.6 reduce-window.6
  8.9 0.2 slice_reduce_fusion
  9.2 0.1 fusion.17
  9.3 0.1 reduce_sum.42
  9.4 0.1 copy.38
  9.5 0.7 multiply_add_fusion
  10.2 0.0 copy-start.8
  10.3 0.6 copy-done.8
  10.9 2.2 convolution_convert_fusion.1
  13.1 5.8 all-to-all-start
  18.9 0.0 copy-done.11
  18.9 0.1 copy.40
  19.0 0.1 mul.83
  19.1 0.0 copy-done.2
  19.2 0.4 mul.85.clone
  19.6 1.1 mul.86
  20.7 0.5 convolution_convert_fusion.2
  21.1 10.0 %all-to-all-done = bf16[8,32,1536]{2,1,0:T(8,128)(2,1)} async-done(((bf16[8,32,1536]{2,1,0:T(8,128)(2,1)}), bf16[8,32,1536]{2,1,0:T(8,128)(2,1)}, u32[]{:S(2)}, u32[]{:S(2)}) %all-to-all-start) | async-done | bytes 786464 | tf_op jit(solution)/shard_map/all_to_all | solution.py:21
  31.2 15.5 %all_to_all.30 = bf16[8,32,1536]{2,1,0:T(8,128)(2,1)S(1)} all-to-all(bf16[8,32,1536]{2,1,0:T(8,128)(2,1)S(1)} %bitcast.68), channel_id=1, replica_groups=mesh['expert'=8,'fsdp'=16] {'expert'}, dimensions={0} | all-to-all | bytes 1572864 | tf_op jit(solution)/shard_map/all_to_all | solution.py:21
  46.7 7.3 %stack.6 = bf16[16,1,8,32,1536]{4,3,2,1,0:T(8,128)(2,1)} broadcast(bf16[8,32,1536]{2,1,0:T(8,128)(2,1)} %all-to-all-done), dimensions={2,3,4} | broadcast | bytes 13369344 | tf_op jit(solution)/shard_map/stack | solution.py:25
  53.9 147.4 %all_to_all.31 = bf16[16,1,8,32,1536]{4,3,2,1,0:T(8,128)(2,1)} all-to-all(bf16[16,1,8,32,1536]{4,3,2,1,0:T(8,128)(2,1)} %stack.6), channel_id=1, replica_groups=mesh['expert'=8,'fsdp'=16] {'fsdp'}, dimensions={0} | all-to-all | bytes 25165824 | tf_op jit(solution)/shard_map/all_to_all | solution.py:24
  201.4 6.1 stack.7
  207.5 5.1 all-to-all-start.4
  212.6 0.2 reduce-scatter.9.cloned.1.call-start
  212.8 0.0 copy-done.1
  212.9 0.0 copy-start.4
  212.9 7.8 %fusion.5 = f32[4096,128]{1,0:T(8,128)} fusion(bf16[4096,1536]{1,0:T(8,128)(2,1)} %bitcast.61, bf16[1,1536,128]{2,1,0:T(8,128)(2,1)S(1)} %copy-done.1), kind=kOutput, calls=%fused_computation.20 | convolution fusion | flops 1610612736 | bytes 15073280 | tf_op jit(solution)/shard_map/dot_general | solution.py:68
  220.7 0.0 copy-done.4
  220.7 7.8 %fusion.9 = f32[4096,128]{1,0:T(8,128)} fusion(bf16[4096,1536]{1,0:T(8,128)(2,1)} %bitcast.62, bf16[1,1536,128]{2,1,0:T(8,128)(2,1)S(1)} %copy-done.4), kind=kOutput, calls=%fused_computation.24 | convolution fusion | flops 1610612736 | bytes 15073280 | tf_op jit(solution)/shard_map/dot_general | solution.py:67
  228.4 165.8 %all-to-all-done.4 = bf16[16,1,8,32,1536]{4,3,2,1,0:T(8,128)(2,1)} async-done(((bf16[16,1,8,32,1536]{4,3,2,1,0:T(8,128)(2,1)}), bf16[16,1,8,32,1536]{4,3,2,1,0:T(8,128)(2,1)}, u32[]{:S(2)}, u32[]{:S(2)}) %all-to-all-start.4) | async-done | bytes 12582944 | tf_op jit(solution)/shard_map/all_to_all | solution.py:24
  394.2 0.0 copy-done
  394.3 9.6 %multiply_convert_fusion = (bf16[4096,128]{1,0:T(8,128)(2,1)S(1)}, bf16[4096,128]{1,0:T(8,128)(2,1)S(1)}, bf16[4096,128]{1,0:T(8,128)(2,1)S(1)}) fusion(f32[4096,128]{1,0:T(8,128)} %fusion.9, f32[4096,128]{1,0:T(8,128)} %fusion.5, bf16[4096,1536]{1,0:T(8,128)(2,1)} %bitcast.12, bf16[1,128,1536]{2,1,0:T(8,128)(2,1)S(1)} %copy-done), kind=kOutput, calls=%fused_computation.8 | convolution fusion | flops 1619001344 | bytes 20316160 | tf_op jit(solution)/shard_map/dot_general | solution.py:79
  403.9 0.0 copy-start.5
  403.9 10.1 %fusion.7 = f32[4096,1536]{1,0:T(8,128)} fusion(bf16[4096,128]{1,0:T(8,128)(2,1)S(1)} %get-tuple-element.9, bf16[1,1536,128]{2,1,0:T(8,128)(2,1)S(1)} %copy-done.4), kind=kOutput, calls=%fused_computation.22 | convolution fusion | flops 1610612736 | bytes 26607616 | tf_op jit(solution)/shard_map/dot_general | solution.py:89
  414.0 0.0 copy-done.5
  414.0 14.7 %add_convert_fusion = bf16[4096,1536]{1,0:T(8,128)(2,1)} fusion(f32[4096,1536]{1,0:T(8,128)} %fusion.7, bf16[4096,128]{1,0:T(8,128)(2,1)S(1)} %get-tuple-element.8, bf16[1,1536,128]{2,1,0:T(8,128)(2,1)S(1)} %copy-done.1), kind=kOutput, calls=%fused_computation | convolution fusion | flops 1623195648 | bytes 39190528 | tf_op jit(solution)/shard_map/dot_general | solution.py:92
  428.7 0.0 reduce-scatter.9.cloned.1.call-update
  428.8 0.3 reduce-scatter.7.cloned.1.call-start
  429.0 6.4 convolution_convert_fusion
  435.4 0.0 reduce-scatter.7.cloned.1.call-update
  435.4 1.0 copy-done.3
  436.4 1.0 convert_element_type.65
  437.3 0.1 iota_compare_fusion.2
  437.5 0.7 eq.68
  438.2 8.0 %convolution_bitcast_fusion.1 = f32[1,1536,128]{2,1,0:T(8,128)} fusion(bf16[4096,1536]{1,0:T(8,128)(2,1)} %bitcast.63, bf16[4096,128]{1,0:T(8,128)(2,1)S(1)} %get-tuple-element.8), kind=kOutput, calls=%fused_computation.5 | convolution fusion | flops 1610612736 | bytes 14417920 | tf_op jit(solution)/shard_map/dot_general | solution.py:88
  446.2 78.4 %reduce-scatter.9.cloned.1.call-done = bf16[1,8,32,1536]{3,2,1,0:T(8,128)(2,1)} async-done(((bf16[16,8,32,1536]{3,2,1,0:T(8,128)(2,1)}), bf16[1,8,32,1536]{3,2,1,0:T(8,128)(2,1)}) %reduce-scatter.9.cloned.1.call-update) | async-done | bytes 786448
  524.6 5.4 all-to-all-start.5
  530.0 0.0 copy-done.6
  530.0 7.3 %convolution_bitcast_fusion.2 = f32[1,1536,128]{2,1,0:T(8,128)} fusion(bf16[4096,1536]{1,0:T(8,128)(2,1)} %bitcast.64, bf16[4096,128]{1,0:T(8,128)(2,1)S(1)} %copy-done.6), kind=kOutput, calls=%fused_computation.6 | convolution fusion | flops 1610612736 | bytes 14417920 | tf_op jit(solution)/shard_map/dot_general | solution.py:85
  537.4 84.8 %reduce-scatter.7.cloned.1.call-done = bf16[1,8,32,1536]{3,2,1,0:T(8,128)(2,1)} async-done(((bf16[16,8,32,1536]{3,2,1,0:T(8,128)(2,1)}), bf16[1,8,32,1536]{3,2,1,0:T(8,128)(2,1)}) %reduce-scatter.7.cloned.1.call-update) | async-done | bytes 786448
  622.2 0.0 all-to-all-done.5
  622.2 5.4 all-to-all-start.2
  627.6 7.4 %convolution_bitcast_fusion = f32[1,128,1536]{2,1,0:T(8,128)} fusion(bf16[4096,128]{1,0:T(8,128)(2,1)S(1)} %get-tuple-element.10, bf16[4096,1536]{1,0:T(8,128)(2,1)} %bitcast.12), kind=kOutput, calls=%fused_computation.4 | convolution fusion | flops 1610612736 | bytes 14417920 | tf_op jit(solution)/shard_map/dot_general | solution.py:84
  635.0 0.0 copy-done.9
  635.0 1.0 convolution_convert_fusion.3
  636.1 3.8 all-to-all-done.2
  639.9 0.0 copy-done.7
  639.9 2.5 multiply_reduce_fusion
  (12 shorter events, 0.1 us)
Async XLA Ops:
  7.2 387.1 %copy-start = (bf16[1,128,1536]{2,1,0:T(8,128)(2,1)S(1)}, bf16[1,128,1536]{2,1,0:T(8,128)(2,1)}, u32[]{:S(2)}) copy-start(bf16[1,128,1536]{2,1,0:T(8,128)(2,1)} %param.13) | copy-start | bytes 1179652
  7.2 11.7 %copy-start.11 = (f32[128,2]{0,1:T(2,128)S(1)}, f32[128,2]{0,1:T(2,128)}, u32[]{:S(2)}) copy-start(f32[128,2]{0,1:T(2,128)} %param.8) | copy-start | bytes 3076
  7.2 12.0 %copy-start.2 = (bf16[128,1536]{1,0:T(8,128)(2,1)S(1)}, bf16[128,1536]{1,0:T(8,128)(2,1)}, u32[]{:S(2)}) copy-start(bf16[128,1536]{1,0:T(8,128)(2,1)} %param.10) | copy-start | bytes 1179652
  10.2 0.6 copy-start.8
  13.1 18.1 %all-to-all-start = ((bf16[8,32,1536]{2,1,0:T(8,128)(2,1)}), bf16[8,32,1536]{2,1,0:T(8,128)(2,1)}, u32[]{:S(2)}, u32[]{:S(2)}) async-start(bf16[8,32,1536]{2,1,0:T(8,128)(2,1)} %bitcast.2), calls=%async_computation | async-start | bytes 1572864 | tf_op jit(solution)/shard_map/all_to_all | solution.py:21
  207.5 5.4 copy-start.1
  207.5 186.8 %all-to-all-start.4 = ((bf16[16,1,8,32,1536]{4,3,2,1,0:T(8,128)(2,1)}), bf16[16,1,8,32,1536]{4,3,2,1,0:T(8,128)(2,1)}, u32[]{:S(2)}, u32[]{:S(2)}) async-start(bf16[16,1,8,32,1536]{4,3,2,1,0:T(8,128)(2,1)} %stack.7), calls=%async_computation.4 | async-start | bytes 25165824 | tf_op jit(solution)/shard_map/all_to_all | solution.py:24
  212.6 312.0 %reduce-scatter.9.cloned.1.call-start = ((), (), s32[]{:S(2)}) async-start(), calls=%async_computation.9 | async-start | bytes 13369344
  212.9 7.8 %copy-start.4 = (bf16[1,1536,128]{2,1,0:T(8,128)(2,1)S(1)}, bf16[1,1536,128]{2,1,0:T(8,128)(2,1)}, u32[]{:S(2)}) copy-start(bf16[1,1536,128]{2,1,0:T(8,128)(2,1)} %param.11) | copy-start | bytes 1179652
  403.9 10.1 %copy-start.5 = (bf16[4096,128]{1,0:T(8,128)(2,1)}, bf16[4096,128]{1,0:T(8,128)(2,1)S(1)}, u32[]{:S(2)}) copy-start(bf16[4096,128]{1,0:T(8,128)(2,1)S(1)} %get-tuple-element.9) | copy-start | bytes 3145732
  428.8 193.4 %reduce-scatter.7.cloned.1.call-start = ((), (), s32[]{:S(2)}) async-start(), calls=%async_computation.8 | async-start | bytes 13369344
  435.4 1.0 copy-start.3
  438.2 91.8 %copy-start.6 = (bf16[4096,128]{1,0:T(8,128)(2,1)S(1)}, bf16[4096,128]{1,0:T(8,128)(2,1)}, u32[]{:S(2)}) copy-start(bf16[4096,128]{1,0:T(8,128)(2,1)} %copy-done.5) | copy-start | bytes 3145732
  524.6 97.6 %all-to-all-start.5 = ((bf16[8,32,1536]{2,1,0:T(8,128)(2,1)}), bf16[8,32,1536]{2,1,0:T(8,128)(2,1)S(1)}, u32[]{:S(2)}, u32[]{:S(2)}) async-start(bf16[8,32,1536]{2,1,0:T(8,128)(2,1)} %bitcast.70), calls=%async_computation.5 | async-start | bytes 1572864 | tf_op jit(solution)/shard_map/all_to_all | solution.py:39
  622.2 17.7 %all-to-all-start.2 = ((bf16[8,32,1536]{2,1,0:T(8,128)(2,1)}), bf16[8,32,1536]{2,1,0:T(8,128)(2,1)}, u32[]{:S(2)}, u32[]{:S(2)}) async-start(bf16[8,32,1536]{2,1,0:T(8,128)(2,1)} %bitcast.69), calls=%async_computation.2 | async-start | bytes 1572864 | tf_op jit(solution)/shard_map/all_to_all | solution.py:39
  627.6 7.4 %copy-start.9 = (bf16[256,128]{1,0:T(8,128)(2,1)S(1)}, bf16[256,128]{1,0:T(8,128)(2,1)}, u32[]{:S(2)}) copy-start(bf16[256,128]{1,0:T(8,128)(2,1)} %copy-done.8) | copy-start | bytes 196612
  627.6 12.3 %copy-start.7 = (f32[128,1536]{1,0:T(8,128)S(1)}, f32[128,1536]{1,0:T(8,128)}, u32[]{:S(2)}) copy-start(f32[128,1536]{1,0:T(8,128)} %convert_element_type.65) | copy-start | bytes 2359300
  627.6 12.3 %copy-start.10 = (pred[128,2,256]{2,1,0:T(4,128)(4,1)S(1)}, pred[128,2,256]{2,1,0:T(4,128)(4,1)}, u32[]{:S(2)}) copy-start(pred[128,2,256]{2,1,0:T(4,128)(4,1)} %eq.68) | copy-start | bytes 196612
Sparse Core Ops, SparseCore 0:
  428.9 95.6 reduce-scatter.8
  528.0 94.1 reduce-scatter.6
